TPU v7x, 512 devices: a whole 4x8x8 slice. The times are simulated.
512 devices in a mesh: lower: 16 (over y, core), upper: 8 (over z), depth: 4 (over x).
Axes of the slice: x: 4, y: 8, z: 8, core: 2. Of those that a mesh axis runs over, the one named last changes fastest.
Arguments:
- lower_vectors: bfloat16 [4, 32768, 2048], P('depth', 'lower', 'upper'), may hold values from -0.0234375 to 0.0234375
- upper_vectors: bfloat16 [4, 32768, 3072], P('depth', 'lower', 'upper'), may hold values from -6 to 6
- energy_lower: float32 [2048], P(('lower', 'depth')), may hold values from 0 to 0.5
- energy_upper: float32 [3072], P('upper'), may hold values from 1 to 2
- sym_lower: int32 [2048], P(('lower', 'depth')), may hold values from 0 to 3
- sym_upper: int32 [3072], P('upper'), may hold values from 0 to 3
- j_lower: int32 [2048], P(('lower', 'depth')), may hold values from 0 to 2
- j_upper: int32 [3072], P('upper'), may hold values from 0 to 2
Outputs:
- einstein: float32 [2048, 3072], P(('lower', 'depth'), 'upper')
All inputs are finite; a program needn't handle non-finite values.
Results may differ from a plain program's by a relative error of at most 0.0003.
Values may be sent and summed in bfloat16 or wider, within the bound.
A program may use at most 64 MiB of HBM per device.

v0:
```python
import jax
import jax.numpy as jnp
from jax import lax
from jax.sharding import PartitionSpec as P


def local(
    lower_vectors, upper_vectors, energy_lower, energy_upper, sym_lower, sym_upper, j_lower, j_upper
):
    lower_rows = lower_vectors[0]
    upper_rows = upper_vectors[0]
    partial_terms = lax.dot_general(
        lax.all_gather(lower_rows, "upper", axis=1, tiled=True),
        upper_rows,
        (((0,), (0,)), ((), ())),
        preferred_element_type=jnp.float32,
    )
    moments = lax.psum_scatter(partial_terms, ("lower", "depth"), scatter_dimension=0, tiled=True)
    parity = sym_lower % 2
    sym_rule = sym_upper[None, :] - sym_lower[:, None] == (1 - 2 * parity)[:, None]
    j_rule = jnp.abs(j_upper[None, :] - j_lower[:, None]) <= 1
    allowed = jnp.logical_and(sym_rule, j_rule)
    frequency = energy_upper[None, :] - energy_lower[:, None]
    weight_upper = (2 * j_upper + 1).astype(jnp.float32)
    value = frequency * frequency * frequency * (moments * moments) / weight_upper[None, :]
    return jnp.where(allowed, value, jnp.zeros_like(value))


def solution(mesh):
    return jax.shard_map(
        local,
        mesh=mesh,
        in_specs=(
            P("depth", "lower", "upper"),
            P("depth", "lower", "upper"),
            P(("lower", "depth")),
            P("upper"),
            P(("lower", "depth")),
            P("upper"),
            P(("lower", "depth")),
            P("upper"),
        ),
        out_specs=P(("lower", "depth"), "upper"),
        check_vma=False,
    )
```

profile of v0, /device:TPU:16, one launch (start us, length us, event | category | flops | bytes accessed | tf_op | source)
XLA Modules:
  0.0 283.6 jit_solution(9405413848341315890)
XLA Ops:
  6.5 0.0 copy-start
  6.5 0.0 all-gather.3.cloned.1.call-start
  6.5 0.7 all-gather.3.cloned.1.call-update
  7.3 0.0 reduce-scatter.2.cloned.1.call-start
  7.3 110.6 %all-gather.3.cloned.1.call-done = bf16[1,2048,2048]{2,1,0:T(8,128)(2,1)} async-done(((bf16[1,2048,256]{2,1,0:T(8,128)(2,1)}), bf16[1,2048,2048]{2,1,0:T(8,128)(2,1)}) %all-gather.3.cloned.1.call-update) | async-done | bytes 8388624 | tf_op jit(solution)/shard_map/all_gather | solution.py:13
  117.9 0.0 copy-done
  117.9 8.7 %fusion = f32[2048,384]{1,0:T(8,128)} fusion(bf16[1,2048,2048]{2,1,0:T(8,128)(2,1)} %all-gather.3.cloned.1.call-done, bf16[1,2048,384]{2,1,0:T(8,128)(2,1)S(1)} %copy-done), kind=kOutput, calls=%fused_computation | convolution fusion | flops 3221225472 | bytes 13107200 | tf_op jit(solution)/shard_map/dot_general | solution.py:12
  126.6 0.0 copy-start.6
  126.6 0.0 copy-start.1
  126.6 0.0 copy-start.2
  126.6 0.0 copy-start.3
  126.7 0.0 copy-start.4
  126.7 0.0 copy-start.5
  126.7 0.0 reduce-scatter.2.cloned.1.call-update
  126.7 0.6 copy-done.6
  127.3 0.0 copy-done.1
  127.3 147.9 %reduce-scatter.2.cloned.1.call-done = f32[32,384]{1,0:T(8,128)} async-done(((f32[2048,384]{1,0:T(8,128)}), f32[32,384]{1,0:T(8,128)}) %reduce-scatter.2.cloned.1.call-update) | async-done | bytes 49168 | tf_op jit(solution)/shard_map/reduce_scatter | solution.py:18
  275.2 0.0 copy-done.2
  275.2 0.0 copy-done.3
  275.2 0.0 copy-done.4
  275.2 0.0 copy-done.5
  275.2 1.5 fusion.5
  (2 shorter events, 0.0 us)
Async XLA Ops:
  6.5 111.4 %copy-start = (bf16[1,2048,384]{2,1,0:T(8,128)(2,1)S(1)}, bf16[1,2048,384]{2,1,0:T(8,128)(2,1)}, u32[]{:S(2)}) copy-start(bf16[1,2048,384]{2,1,0:T(8,128)(2,1)} %param.9) | copy-start | bytes 4718596
  6.5 111.4 %all-gather.3.cloned.1.call-start = ((), (), s32[]{:S(2)}) async-start(), calls=%async_computation.2 | async-start | bytes 9437184 | tf_op jit(solution)/shard_map/all_gather | solution.py:13
  7.3 268.0 %reduce-scatter.2.cloned.1.call-start = ((), (), s32[]{:S(2)}) async-start(), calls=%async_computation.1 | async-start | bytes 3194880 | tf_op jit(solution)/shard_map/reduce_scatter | solution.py:18
  126.6 0.7 copy-start.6
  126.6 0.7 copy-start.1
  126.6 148.6 %copy-start.2 = (f32[384]{0:T(512)S(1)}, f32[384]{0:T(512)}, u32[]{:S(2)}) copy-start(f32[384]{0:T(512)} %param.11) | copy-start | bytes 4612
  126.6 148.6 %copy-start.3 = (s32[384]{0:T(512)S(1)}, s32[384]{0:T(512)}, u32[]{:S(2)}) copy-start(s32[384]{0:T(512)} %param.13) | copy-start | bytes 4612
  126.7 148.6 %copy-start.4 = (f32[32]{0:T(128)S(1)}, f32[32]{0:T(128)}, u32[]{:S(2)}) copy-start(f32[32]{0:T(128)} %param.10) | copy-start | bytes 388
  126.7 148.6 %copy-start.5 = (s32[32]{0:T(128)S(1)}, s32[32]{0:T(128)}, u32[]{:S(2)}) copy-start(s32[32]{0:T(128)} %param.14) | copy-start | bytes 388
Sparse Core Ops, SparseCore 0:
  9.4 108.5 all-gather.2
  126.8 148.3 reduce-scatter.1
where the time goes:
time: 284 us
  waiting for transfers between devices  259 us (91%)
  between operations  13.4 us (5%)
  matrix products  8.69 us (3%)
    reduce_scatter x1, waiting for transfers between devices, local(): lax.psum_scatter(partial_terms, ('lower', 'depth'), scatter_dimension=0,...  148 us
    all_gather x1, waiting for transfers between devices, local(): lax.all_gather(lower_rows, 'upper', axis=1, tiled=True)  111 us
    dot_general x1, matrix products, local(): lax.dot_general(lax.all_gather(lower_rows, 'upper', axis=1, tiled=True),...  8.69 us
  transfers between devices with their start and end apart: 2, of which 2 were waited for; matrix products, arithmetic and copies ran while one was open for 0% of the time, Pallas kernels for 0%

commit v1 on v0

--- a/solution.py
+++ b/solution.py
@@ -9,8 +9,15 @@
 ):
     lower_rows = lower_vectors[0]
     upper_rows = upper_vectors[0]
+
+    def build_groups_here(point, dim_at):
+        left_arr = jax.lax.axis_size("upper")
+        a_next = jnp.stack([point] * left_arr, 0)
+        inter = jax.lax.all_to_all(a_next, axis_name="upper", split_axis=0, concat_axis=0)
+        return jnp.concatenate(inter, dim_at)
+
     partial_terms = lax.dot_general(
-        lax.all_gather(lower_rows, "upper", axis=1, tiled=True),
+        build_groups_here(lower_rows, 1),
         upper_rows,
         (((0,), (0,)), ((), ())),
         preferred_element_type=jnp.float32,

time: 284 us -> 367 us (1.29)
  blocking collectives: 0 us -> 196 us
  waiting for transfers between devices: 259 us -> 146 us
    all_to_all x0 -> x1, blocking collectives: none -> 196 us  [build_groups_here(): jax.lax.all_to_all(a_next, axis_name='upper', split_axis=0, concat_axis=0)]
    all_gather x1 -> x0, waiting for transfers between devices: 111 us -> none  [local(): lax.all_gather(lower_rows, 'upper', axis=1, tiled=True)]
  transfers between devices with their start and end apart: 2 -> 1, of which waited for: 2 -> 1; matrix products, arithmetic and copies ran while one was open for 0% -> 0% of each run, Pallas kernels for 0% -> 0%
where the time goes in v1:
time: 367 us; the launch traced here: 366 us
  blocking collectives  196 us (53%)
  waiting for transfers between devices  146 us (40%)
  between operations  13.4 us (4%)
  matrix products  6.3 us (2%)
    all_to_all x1, blocking collectives, build_groups_here(): jax.lax.all_to_all(a_next, axis_name='upper', split_axis=0, concat_axis=0)  196 us
    reduce_scatter x1, waiting for transfers between devices, local(): lax.psum_scatter(partial_terms, ('lower', 'depth'), scatter_dimension=0,...  146 us
  transfers between devices with their start and end apart: 1, of which 1 were waited for; matrix products, arithmetic and copies ran while one was open for 0% of the time, Pallas kernels for 0%

profile of v1, /device:TPU:16, one launch (start us, length us, event | category | flops | bytes accessed | tf_op | source)
XLA Modules:
  0.0 366.4 jit_solution(10670705558311870633)
XLA Ops:
  6.5 0.0 copy-start
  6.5 0.0 reduce-scatter.2.cloned.1.call-start
  6.5 1.6 copy.9
  8.1 1.1 stack.3
  9.2 196.1 %all_to_all.5 = bf16[8,2048,256]{1,2,0:T(8,128)(2,1)S(1)} all-to-all(bf16[8,2048,256]{1,2,0:T(8,128)(2,1)S(1)} %stack.3), channel_id=1, replica_groups=mesh['lower'=16,'upper'=8,'depth'=4] {'upper'}, dimensions={0} | all-to-all | bytes 16777216 | tf_op jit(solution)/shard_map/all_to_all | solution.py:16
  205.3 0.0 copy-done
  205.3 6.3 %fusion = f32[2048,384]{1,0:T(8,128)} fusion(bf16[2048,2048]{0,1:T(8,128)(2,1)S(1)} %bitcast.8, bf16[1,2048,384]{2,1,0:T(8,128)(2,1)S(1)} %copy-done), kind=kOutput, calls=%fused_computation | convolution fusion | flops 3221225472 | bytes 13107200 | tf_op jit(solution)/shard_map/dot_general | solution.py:19
  211.6 0.0 copy-start.6
  211.7 0.0 copy-start.1
  211.7 0.0 copy-start.2
  211.7 0.0 copy-start.3
  211.7 0.0 copy-start.4
  211.7 0.0 copy-start.5
  211.7 0.0 reduce-scatter.2.cloned.1.call-update
  211.7 0.6 copy-done.6
  212.3 0.0 copy-done.1
  212.4 145.6 %reduce-scatter.2.cloned.1.call-done = f32[32,384]{1,0:T(8,128)} async-done(((f32[2048,384]{1,0:T(8,128)}), f32[32,384]{1,0:T(8,128)}) %reduce-scatter.2.cloned.1.call-update) | async-done | bytes 49168 | tf_op jit(solution)/shard_map/reduce_scatter | solution.py:25
  358.0 0.0 copy-done.2
  358.0 0.0 copy-done.3
  358.0 0.0 copy-done.4
  358.0 0.0 copy-done.5
  358.0 1.5 fusion.4
  (2 shorter events, 0.0 us)
Async XLA Ops:
  6.5 198.8 %copy-start = (bf16[1,2048,384]{2,1,0:T(8,128)(2,1)S(1)}, bf16[1,2048,384]{2,1,0:T(8,128)(2,1)}, u32[]{:S(2)}) copy-start(bf16[1,2048,384]{2,1,0:T(8,128)(2,1)} %param.9) | copy-start | bytes 4718596
  6.5 351.4 %reduce-scatter.2.cloned.1.call-start = ((), (), s32[]{:S(2)}) async-start(), calls=%async_computation.2 | async-start | bytes 3194880 | tf_op jit(solution)/shard_map/reduce_scatter | solution.py:25
  211.6 0.7 copy-start.6
  211.7 0.7 copy-start.1
  211.7 146.3 %copy-start.2 = (f32[384]{0:T(512)S(1)}, f32[384]{0:T(512)}, u32[]{:S(2)}) copy-start(f32[384]{0:T(512)} %param.11) | copy-start | bytes 4612
  211.7 146.3 %copy-start.3 = (s32[384]{0:T(512)S(1)}, s32[384]{0:T(512)}, u32[]{:S(2)}) copy-start(s32[384]{0:T(512)} %param.13) | copy-start | bytes 4612
  211.7 146.3 %copy-start.4 = (f32[32]{0:T(128)S(1)}, f32[32]{0:T(128)}, u32[]{:S(2)}) copy-start(f32[32]{0:T(128)} %param.10) | copy-start | bytes 388
  211.7 146.3 %copy-start.5 = (s32[32]{0:T(128)S(1)}, s32[32]{0:T(128)}, u32[]{:S(2)}) copy-start(s32[32]{0:T(128)} %param.14) | copy-start | bytes 388
Sparse Core Ops, SparseCore 0:
  211.8 146.1 reduce-scatter.1
